TPU v7x, 128 devices: a whole 4x4x4 slice. The times are simulated.
128 devices in a mesh: orow: 16 (over z, x), ocol: 8 (over y, core).
Axes of the slice: x: 4, y: 4, z: 4, core: 2. Of those that a mesh axis runs over, the one named last changes fastest.
Arguments:
- integrals: bfloat16 [2304, 32, 384], P('ocol', 'orow'), may hold values from -0.29882812 to 0.29882812
- occ_count: int32 [16], replicated, may hold values from 1 to 2
- occ_energy: float32 [32], replicated, may hold values from -2 to -0.5
- vir_energy: float32 [384], replicated, may hold values from 0.3 to 2.5
- task_iblock: int32 [64, 1], replicated, may hold values from 0 to 15; in each aligned block of 64 rows (0 to 63, 64 to 127, ...) at most 8 rows name the same one
- task_jblock: int32 [64], replicated, may hold values from 0 to 15
Outputs:
- gamma_out: float32 [2304, 32, 384], P('ocol', 'orow')
- density: float32 [384, 384], replicated
Inputs may be any that keep to these rules, and one draw needn't show every extreme that they name: `task_iblock`: no first block is named by more than 8 tasks, and some first block by exactly 8.
All inputs are finite; a program needn't handle non-finite values.
Results may differ from a plain program's by a relative error of at most 0.0019.
Values may be sent and summed in bfloat16 or wider, within the bound.
No kernel may reach another device: no remote copies, remote signals or barrier semaphores. Data moves between devices by JAX's collectives and lax.ppermute only.
A program may use at most 128 MiB of HBM per device.

v0:
```python
import jax
import jax.numpy as jnp
from jax import lax
from jax.sharding import Mesh
from jax.sharding import PartitionSpec as P

OROW = ("orow_0", "orow_1")
OCOL = ("ocol_0", "ocol_1")
OROW_OCOL = ("orow_0", "orow_1", "ocol_0", "ocol_1")


def rows_for(lines, length):
    spare = -lines.shape[0] % length
    if not spare:
        return lines
    return jnp.concatenate([lines, jnp.zeros((spare, *lines.shape[1:]), lines.dtype)])


def sum_in_order(pieces, axes, turns):
    lengths = [lax.axis_size(a) for a in axes]
    pieces = pieces.reshape(*lengths, *pieces.shape[1:])
    pieces = pieces.transpose(*turns, *range(len(axes), pieces.ndim))
    pieces = pieces.reshape(-1, *pieces.shape[len(axes) :])
    for k in turns:
        pieces = lax.psum_scatter(pieces, axes[k], scatter_dimension=0, tiled=True)
    return pieces[0]


def gather_in_order(x, axes, turns):
    pieces = x
    for k in turns:
        pieces = lax.all_gather(pieces, axes[k])
    done = turns[::-1]
    back = [done.index(k) for k in range(len(axes))]
    pieces = pieces.transpose(*back, *range(len(axes), pieces.ndim))
    return pieces.reshape(-1, *x.shape)


def total_of(x, axes, turns):
    length, lines = (lax.axis_size(axes), x.reshape(-1, *x.shape[1:][-1:]))
    pieces = rows_for(lines, length).reshape(length, -1, *lines.shape[1:])
    own = sum_in_order(pieces, axes, turns)
    whole = gather_in_order(own, axes, turns[::-1]).reshape(-1, *lines.shape[1:])
    return whole[: len(lines)].reshape(x.shape)


def make_amplitudes(k_total, i_energy, j_energy, vir_energy, usable):
    slots = k_total.shape[0]
    orbitals = i_energy.shape[1]
    virtuals = vir_energy.shape[0]
    k_grid = k_total.reshape(slots, orbitals, virtuals, orbitals, virtuals)
    denominator = (
        i_energy[:, :, None, None, None]
        + j_energy[:, None, None, :, None]
        - vir_energy[None, None, :, None, None]
        - vir_energy[None, None, None, None, :]
    )
    values = (2.0 * k_grid - jnp.swapaxes(k_grid, 2, 4)) / denominator
    values = values * usable[:, None, None, None, None]
    return values.astype(jnp.bfloat16).reshape(slots, orbitals * virtuals, orbitals * virtuals)


def local(integrals, occ_count, occ_energy, vir_energy, task_iblock, task_jblock):
    aux_local = integrals.shape[0]
    orbitals = integrals.shape[1]
    virtuals = integrals.shape[2]
    span = orbitals * virtuals
    block_total = lax.axis_size(OROW)
    col_total = lax.axis_size(OCOL)
    my_row = lax.axis_index(OROW)
    my_col = lax.axis_index(OCOL)
    active = jnp.arange(orbitals) < occ_count[my_row]
    masked = integrals * active.astype(jnp.bfloat16)[None, :, None]
    gathered = lax.all_gather(masked, OROW, axis=1, tiled=True)
    flat_blocks = gathered.reshape(aux_local, block_total, span)
    first_list = task_iblock[:, 0]
    task_total = first_list.shape[0]
    per_row = task_total // block_total
    task_ids = my_row * per_row + jnp.arange(per_row)
    i_block = first_list[task_ids]
    j_block = task_jblock[task_ids]
    usable = jnp.ones((per_row,), jnp.float32)
    energy_grid = occ_energy.reshape(block_total, orbitals)
    i_rows = jnp.take(flat_blocks, i_block, axis=1)
    j_rows = jnp.take(flat_blocks, j_block, axis=1)
    k_partial = jnp.einsum("psx,psy->sxy", i_rows, j_rows, preferred_element_type=jnp.float32)
    slots = k_partial.shape[0]
    i_energy = energy_grid[i_block]
    j_energy = energy_grid[j_block]
    k_total = lax.psum(k_partial, OCOL)
    amplitudes = make_amplitudes(k_total, i_energy, j_energy, vir_energy, usable)
    gamma_i = jnp.einsum("sxy,psy->psx", amplitudes, j_rows, preferred_element_type=jnp.float32)
    gamma_j = jnp.einsum("sxy,psx->psy", amplitudes, i_rows, preferred_element_type=jnp.float32)
    slice_width = span // col_total
    amp_grid = amplitudes.reshape(slots, orbitals, virtuals, span)
    column_part = lax.dynamic_slice_in_dim(amp_grid, my_col * slice_width, slice_width, 3)
    dens_part = jnp.einsum(
        "siaw,sibw->ab", column_part, column_part, preferred_element_type=jnp.float32
    )
    block_ids = jnp.arange(block_total)
    i_onehot = (i_block[:, None] == block_ids[None, :]).astype(jnp.float32)
    j_onehot = (j_block[:, None] == block_ids[None, :]).astype(jnp.float32)
    buffer = jnp.einsum(
        "sk,psx->pkx", i_onehot, gamma_i, precision=lax.Precision.HIGHEST
    ) + jnp.einsum("sk,psx->pkx", j_onehot, gamma_j, precision=lax.Precision.HIGHEST)
    owned = lax.psum_scatter(buffer, OROW, scatter_dimension=1, tiled=True)
    gamma_out = owned.reshape(aux_local, orbitals, virtuals)
    density = total_of(dens_part, OROW_OCOL, (0, 1, 2, 3)) / task_total
    return (gamma_out, density)


def solution(mesh):
    finer = Mesh(mesh.devices.reshape(4, 4, 4, 2), ("orow_0", "orow_1", "ocol_0", "ocol_1"))
    placed = (P(OCOL, OROW, None), P(), P(), P(), P(), P())
    return jax.shard_map(
        local, mesh=finer, in_specs=placed, out_specs=(P(OCOL, OROW, None), P()), check_vma=False
    )
```

profile of v0, /device:TPU:1, one launch (start us, length us, event | category | flops | bytes accessed | tf_op | source)
XLA Modules:
  0.0 520.0 jit_solution(48696897312067520)
XLA Ops:
  9.1 1.9 copy_multiply_fusion.1
  13.1 66.1 %all-gather.5.cloned.1.call-done = bf16[288,32,384]{2,0,1:T(8,128)(2,1)} async-done(((bf16[288,2,384]{2,0,1:T(8,128)(2,1)}), bf16[288,32,384]{2,0,1:T(8,128)(2,1)}) %all-gather.5.cloned.1.call-update) | async-done | bytes 7077904 | tf_op jit(solution)/shard_map/all_gather | solution.py:74
  79.2 8.5 %copy.47 = bf16[288,32,384]{2,1,0:T(8,128)(2,1)} copy(bf16[288,32,384]{2,0,1:T(8,128)(2,1)} %all-gather.5.cloned.1.call-done) | data formatting | bytes 14155776 | tf_op jit(solution)/shard_map/all_gather | solution.py:74
  87.8 11.3 %reshape.91 = bf16[288,16,768]{2,1,0:T(8,128)(2,1)} reshape(bf16[288,32,384]{2,1,0:T(8,128)(2,1)} %copy.47) | data formatting | bytes 14155776 | tf_op jit(solution)/shard_map/reshape | solution.py:75
  99.1 8.3 %copy.48 = bf16[288,16,768]{2,0,1:T(8,128)(2,1)} copy(bf16[288,16,768]{2,1,0:T(8,128)(2,1)} %reshape.91) | data formatting | bytes 14155776 | tf_op jit(solution)/shard_map/reshape | solution.py:75
  107.4 3.7 gather_fusion.5
  111.1 3.7 gather_fusion.4
  114.8 5.2 fusion.6
  120.0 12.5 %reshape.92 = f32[4,2,384,2,384]{4,3,2,1,0:T(2,128)} reshape(f32[4,768,768]{2,1,0:T(8,128)} %fusion.6) | data formatting | bytes 18874368 | tf_op jit(solution)/shard_map/reshape | solution.py:51
  132.5 14.8 %copy.50 = f32[4,2,384,2,384]{2,4,3,1,0:T(8,128)} copy(f32[4,2,384,2,384]{4,3,2,1,0:T(2,128)} %reshape.92) | data formatting | bytes 18874368 | tf_op jit(solution)/shard_map/reshape | solution.py:51
  157.6 103.2 %all-reduce.9.cloned.1.call-done = f32[4,2,384,2,384]{2,4,3,1,0:T(8,128)} async-done(((f32[4,2,384,2,384]{2,4,3,1,0:T(8,128)}), f32[4,2,384,2,384]{2,4,3,1,0:T(8,128)}) %all-reduce.9.cloned.1.call-update) | async-done | bytes 9437200 | tf_op jit(solution)/shard_map/psum | solution.py:90
  260.8 9.6 %copy.51 = f32[4,2,384,2,384]{4,2,3,1,0:T(8,128)} copy(f32[4,2,384,2,384]{2,4,3,1,0:T(8,128)} %all-reduce.9.cloned.1.call-done) | data formatting | bytes 18874368 | tf_op jit(solution)/shard_map/psum | solution.py:90
  270.4 9.6 %fusion.1 = bf16[4,2,384,2,384]{4,2,3,1,0:T(8,128)(2,1)} fusion(f32[4,2,384,2,384]{2,4,3,1,0:T(8,128)} %all-reduce.9.cloned.1.call-done, f32[4,2,384,2,384]{4,2,3,1,0:T(8,128)} %copy.51, f32[384]{0:T(512)S(1)} %copy-done.2, f32[4,2,384,2]{2,3,1,0:T(2,128)} %broadcast_subtract_fusion), kind=kLoop, calls=%fused_computation.9 | loop fusion | flops 11796480 | bytes 23619072 | tf_op jit(solution)/shard_map/convert_element_type | solution.py:60
  280.0 6.7 %copy.63 = bf16[4,2,384,2,384]{2,4,3,0,1:T(8,128)(2,1)} copy(bf16[4,2,384,2,384]{4,2,3,1,0:T(8,128)(2,1)} %fusion.1) | data formatting | bytes 9437184 | tf_op jit(solution)/shard_map/reshape;reshape | solution.py:95
  286.7 9.4 %copy.52 = bf16[4,2,384,2,384]{4,3,2,1,0:T(2,128)(2,1)} copy(bf16[4,2,384,2,384]{4,2,3,1,0:T(8,128)(2,1)} %fusion.1) | data formatting | bytes 9437184 | tf_op jit(solution)/shard_map/convert_element_type | solution.py:60
  296.1 11.4 %reshape.94 = bf16[4,768,768]{2,1,0:T(8,128)(2,1)} reshape(bf16[4,2,384,2,384]{4,3,2,1,0:T(2,128)(2,1)} %copy.52) | data formatting | bytes 9437184 | tf_op jit(solution)/shard_map/reshape | solution.py:60
  307.5 2.6 convolution_bitcast_fusion.2
  310.0 2.2 reshape_reshape_reshape.3
  312.5 4.0 convolution_bitcast_fusion.1
  316.5 9.7 %fusion.3 = f32[288,768,16]{1,2,0:T(8,128)} fusion(f32[288,4,768]{2,0,1:T(8,128)S(1)} %convolution_bitcast_fusion.1, s32[4]{0:T(128)S(1)} %copy-done.4), kind=kOutput, calls=%fused_computation.11 | convolution fusion | flops 169869376 | bytes 17694736 | tf_op jit(solution)/shard_map/sk,psx->pkx/dot_general | solution.py:103
  326.2 3.3 convolution_bitcast_fusion
  329.5 25.9 %all-reduce.11.cloned.1.call-done = f32[128,3,384]{2,1,0:T(4,128)} async-done(((f32[128,3,384]{2,1,0:T(4,128)}), f32[128,3,384]{2,1,0:T(4,128)}) %all-reduce.11.cloned.1.call-update) | async-done | bytes 589840
  357.1 15.3 %add_bitcast_fusion = f32[288,16,768]{2,1,0:T(8,128)} fusion(f32[288,768,16]{1,2,0:T(8,128)} %fusion.3, f32[288,4,768]{2,0,1:T(8,128)} %convolution_bitcast_fusion, s32[4]{0:T(128)S(1)} %copy-done.6), kind=kOutput, calls=%fused_computation.6 | convolution fusion | flops 173408320 | bytes 31850512 | tf_op jit(solution)/shard_map/sk,psx->pkx/dot_general | solution.py:105
  372.4 18.3 %copy.55 = f32[288,16,768]{2,0,1:T(8,128)} copy(f32[288,16,768]{2,1,0:T(8,128)} %add_bitcast_fusion) | data formatting | bytes 28311552 | tf_op jit(solution)/shard_map/add | solution.py:103
  394.4 5.8 %all-reduce.13.cloned.1.call-done = f32[32,3,384]{2,1,0:T(4,128)} async-done(((f32[32,3,384]{2,1,0:T(4,128)}), f32[32,3,384]{2,1,0:T(4,128)}) %all-reduce.13.cloned.1.call-update) | async-done | bytes 147472
  401.0 14.0 %all-reduce.3 = f32[8,3,384]{2,1,0:T(4,128)S(1)} all-reduce(f32[8,3,384]{2,1,0:T(4,128)S(1)} %constant_dynamic-slice_fusion.1), channel_id=8, replica_groups=mesh['orow_0'=4,'orow_1'=4,'ocol_0'=4,'ocol_1'=2] {'ocol_0'}, use_global_device_ids=true, to_apply=%region_4.6.clone | all-reduce | flops 9216 | bytes 73728
  415.0 9.2 %all-reduce.4 = f32[2,3,384]{2,1,0:T(4,128)S(1)} all-reduce(f32[2,3,384]{2,1,0:T(4,128)S(1)} %constant_dynamic-slice_fusion), channel_id=9, replica_groups=mesh['orow_0'=4,'orow_1'=4,'ocol_0'=4,'ocol_1'=2] {'ocol_1'}, use_global_device_ids=true, to_apply=%region_5.7.clone | all-reduce | flops 2304 | bytes 18432
  426.7 10.1 %all-gather = f32[8,3,384]{2,1,0:T(4,128)S(1)} all-gather(f32[2,3,384]{2,1,0:T(4,128)S(1)} %all_gather.25), channel_id=2, replica_groups=mesh['orow_0'=4,'orow_1'=4,'ocol_0'=4,'ocol_1'=2] {'ocol_0'}, dimensions={0}, use_global_device_ids=true | all-gather | bytes 46080 | tf_op jit(solution)/shard_map/all_gather | solution.py:32
  436.9 11.4 %all-gather.1 = f32[16,2,3,384]{3,1,2,0:T(2,128)S(1)} all-gather(f32[4,2,3,384]{3,1,2,0:T(2,128)S(1)} %copy.58), channel_id=3, replica_groups=mesh['orow_0'=4,'orow_1'=4,'ocol_0'=4,'ocol_1'=2] {'orow_1'}, dimensions={0}, use_global_device_ids=true | all-gather | bytes 184320 | tf_op jit(solution)/shard_map/all_gather | solution.py:32
  448.3 14.9 %all-gather.2 = f32[16,4,2,3,384]{4,1,3,2,0:T(4,128)S(1)} all-gather(f32[4,4,2,3,384]{4,1,3,2,0:T(4,128)S(1)} %copy.59), channel_id=4, replica_groups=mesh['orow_0'=4,'orow_1'=4,'ocol_0'=4,'ocol_1'=2] {'orow_0'}, dimensions={0}, use_global_device_ids=true | all-gather | bytes 737280 | tf_op jit(solution)/shard_map/all_gather | solution.py:32
  464.7 46.0 %reduce-scatter.4.cloned.1.call-done = f32[288,1,768]{2,0,1:T(8,128)} async-done(((f32[288,16,768]{2,0,1:T(8,128)}), f32[288,1,768]{2,0,1:T(8,128)}) %reduce-scatter.4.cloned.1.call-update) | async-done | bytes 884752
  510.7 2.6 reshape.95
  (69 shorter events, 22.8 us)
Async XLA Ops:
  7.2 4.0 copy-start
  7.2 72.1 %all-gather.5.cloned.1.call-start = ((), (), s32[]{:S(2)}) async-start(), calls=%async_computation.1 | async-start | bytes 7520256 | tf_op jit(solution)/shard_map/all_gather | solution.py:74
  11.0 249.8 %all-reduce.9.cloned.1.call-start = ((), (), s32[]{:S(2)}) async-start(), calls=%async_computation.2 | async-start | bytes 18874368 | tf_op jit(solution)/shard_map/psum | solution.py:90
  11.8 76.0 %copy-start.3 = (s32[4]{0:T(128)}, s32[4]{0:T(128)S(1)}, u32[]{:S(2)}) copy-start(s32[4]{0:T(128)S(1)} %gather_fusion.1) | copy-start | bytes 52
  13.1 74.7 %copy-start.5 = (s32[4]{0:T(128)}, s32[4]{0:T(128)S(1)}, u32[]{:S(2)}) copy-start(s32[4]{0:T(128)S(1)} %gather_fusion) | copy-start | bytes 52
  147.3 208.0 %all-reduce.11.cloned.1.call-start = ((), (), s32[]{:S(2)}) async-start(), calls=%async_computation.3 | async-start | bytes 1572864
  157.6 112.8 %copy-start.2 = (f32[384]{0:T(512)S(1)}, f32[384]{0:T(512)}, u32[]{:S(2)}) copy-start(f32[384]{0:T(512)} %param.11) | copy-start | bytes 4612
  312.3 4.2 copy-start.4
  312.3 87.9 %all-reduce.13.cloned.1.call-start = ((), (), s32[]{:S(2)}) async-start(), calls=%async_computation.4 | async-start | bytes 393216
  312.5 13.7 %slice-start = ((s8[4718592]{0:T(1024)(128)(4,1)}), s8[524288]{0:T(1024)(128)(4,1)S(1)}, s32[]{:S(2)}) async-start(s8[4718592]{0:T(1024)(128)(4,1)} %bitcast.58), calls=%async_computation.6 | async-start | bytes 1048576
  316.5 9.7 %slice-start.1 = ((s8[4718592]{0:T(1024)(128)(4,1)}), s8[4194304]{0:T(1024)(128)(4,1)S(1)}, s32[]{:S(2)}) async-start(s8[4718592]{0:T(1024)(128)(4,1)} %bitcast.58), calls=%async_computation.7 | async-start | bytes 8388608
  326.2 30.9 %copy-start.6 = (s32[4]{0:T(128)S(1)}, s32[4]{0:T(128)}, u32[]{:S(2)}) copy-start(s32[4]{0:T(128)} %copy-done.5) | copy-start | bytes 52
  357.0 153.6 %reduce-scatter.4.cloned.1.call-start = ((), (), s32[]{:S(2)}) async-start(), calls=%async_computation.5 | async-start | bytes 15040512
  390.7 0.7 copy-start.9
  390.7 1.2 copy-start.8
  390.7 1.9 copy-start.7
  391.3 121.9 %copy-start.1 = (s32[64,1]{0,1:T(1,128)S(1)}, s32[64,1]{0,1:T(1,128)}, u32[]{:S(2)}) copy-start(s32[64,1]{0,1:T(1,128)} %param.12) | copy-start | bytes 772
Sparse Core Ops, SparseCore 0:
  11.2 68.0 all-gather.4
  147.5 113.3 all-reduce.8
  312.4 42.9 all-reduce.10
  358.1 42.0 all-reduce.12
  403.6 107.0 reduce-scatter.3
where the time goes:
time: 529 us; the launch traced here: 520 us
  waiting for transfers between devices  247 us (47%)
  local copies, waits for them, and re-layouts  138 us (26%)
  blocking collectives  61.5 us (12%)
  matrix products  40 us (8%)
  other arithmetic  16.9 us (3%)
  between operations  16.2 us (3%)
    psum x1, waiting for transfers between devices, local(): k_total = lax.psum(k_partial, OCOL)  103 us
    unnamed x8, waiting for transfers between devices  77.7 us
    all_gather x1, waiting for transfers between devices, local(): gathered = lax.all_gather(masked, OROW, axis=1, tiled=True)  66.1 us
    all_gather x4, blocking collectives, gather_in_order(): pieces = lax.all_gather(pieces, axes[k])  38.2 us
    reshape x2, local copies, waits for them, and re-layouts, make_amplitudes(): k_grid = k_total.reshape(slots, orbitals, virtuals, orbitals, virtuals)  27.3 us
    unnamed x2, blocking collectives  23.3 us
    reshape x2, local copies, waits for them, and re-layouts, local(): flat_blocks = gathered.reshape(aux_local, block_total, span)  19.6 us
    add x1, local copies, waits for them, and re-layouts, local(): jnp.einsum('sk,psx->pkx', i_onehot, gamma_i, precision=lax.Precision.HIGH...  18.3 us
  transfers between devices with their start and end apart: 5, of which 5 were waited for; matrix products, arithmetic and copies ran while one was open for 13% of the time, Pallas kernels for 0%

commit v1 on v0

--- a/solution.py
+++ b/solution.py
@@ -7,6 +7,7 @@
 OROW = ("orow_0", "orow_1")
 OCOL = ("ocol_0", "ocol_1")
 OROW_OCOL = ("orow_0", "orow_1", "ocol_0", "ocol_1")
+step_on_signs = lambda load: jnp.sum(lax.all_gather(load, OCOL), 0)
 
 
 def rows_for(lines, length):
@@ -87,7 +88,7 @@
     slots = k_partial.shape[0]
     i_energy = energy_grid[i_block]
     j_energy = energy_grid[j_block]
-    k_total = lax.psum(k_partial, OCOL)
+    k_total = step_on_signs(k_partial)
     amplitudes = make_amplitudes(k_total, i_energy, j_energy, vir_energy, usable)
     gamma_i = jnp.einsum("sxy,psy->psx", amplitudes, j_rows, preferred_element_type=jnp.float32)
     gamma_j = jnp.einsum("sxy,psx->psy", amplitudes, i_rows, preferred_element_type=jnp.float32)

time: 529 us -> 770 us (1.46)
  waiting for transfers between devices: 247 us -> 464 us
  other arithmetic: 16.9 us -> 45.5 us
  local copies, waits for them, and re-layouts: 138 us -> 127 us
    all_gather x0 -> x1, waiting for transfers between devices: none -> 324 us  [step_on_signs = lambda load: jnp.sum(lax.all_gather(load, OCOL), 0)]
    psum x1 -> x0, waiting for transfers between devices: 103 us -> none  [local(): k_total = lax.psum(k_partial, OCOL)]
    reduce_sum x0 -> x1, other arithmetic: none -> 28.2 us  [step_on_signs = lambda load: jnp.sum(lax.all_gather(load, OCOL), 0)]
    psum x1 -> x0, local copies, waits for them, and re-layouts: 9.6 us -> none  [local(): k_total = lax.psum(k_partial, OCOL)]
  transfers between devices with their start and end apart: 5 -> 5, of which waited for: 5 -> 5; matrix products, arithmetic and copies ran while one was open for 13% -> 9% of each run, Pallas kernels for 0% -> 0%
where the time goes in v1:
time: 770 us; the launch traced here: 762 us
  waiting for transfers between devices  464 us (60%)
  local copies, waits for them, and re-layouts  127 us (16%)
  blocking collectives  61.5 us (8%)
  matrix products  47 us (6%)
  other arithmetic  45.5 us (6%)
  between operations  16.1 us (2%)
    all_gather x1, waiting for transfers between devices, step_on_signs = lambda load: jnp.sum(lax.all_gather(load, OCOL), 0)  324 us
    unnamed x8, waiting for transfers between devices  74.1 us
    all_gather x1, waiting for transfers between devices, local(): gathered = lax.all_gather(masked, OROW, axis=1, tiled=True)  66.1 us
    all_gather x4, blocking collectives, gather_in_order(): pieces = lax.all_gather(pieces, axes[k])  38.2 us
    reduce_sum x1, other arithmetic, step_on_signs = lambda load: jnp.sum(lax.all_gather(load, OCOL), 0)  28.2 us
    reshape x2, local copies, waits for them, and re-layouts, make_amplitudes(): k_grid = k_total.reshape(slots, orbitals, virtuals, orbitals, virtuals)  27.3 us
    unnamed x2, blocking collectives  23.3 us
    reshape x2, local copies, waits for them, and re-layouts, local(): flat_blocks = gathered.reshape(aux_local, block_total, span)  19.6 us
  transfers between devices with their start and end apart: 5, of which 5 were waited for; matrix products, arithmetic and copies ran while one was open for 9% of the time, Pallas kernels for 0%

profile of v1, /device:TPU:1, one launch (start us, length us, event | category | flops | bytes accessed | tf_op | source)
XLA Modules:
  0.0 761.7 jit_solution(11132989784302936038)
XLA Ops:
  9.1 1.9 copy_multiply_fusion.2
  13.1 66.1 %all-gather.7.cloned.1.call-done = bf16[288,32,384]{2,0,1:T(8,128)(2,1)} async-done(((bf16[288,2,384]{2,0,1:T(8,128)(2,1)}), bf16[288,32,384]{2,0,1:T(8,128)(2,1)}) %all-gather.7.cloned.1.call-update) | async-done | bytes 7077904 | tf_op jit(solution)/shard_map/all_gather | solution.py:75
  79.2 8.5 %copy.48 = bf16[288,32,384]{2,1,0:T(8,128)(2,1)} copy(bf16[288,32,384]{2,0,1:T(8,128)(2,1)} %all-gather.7.cloned.1.call-done) | data formatting | bytes 14155776 | tf_op jit(solution)/shard_map/all_gather | solution.py:75
  87.8 11.3 %reshape.91 = bf16[288,16,768]{2,1,0:T(8,128)(2,1)} reshape(bf16[288,32,384]{2,1,0:T(8,128)(2,1)} %copy.48) | data formatting | bytes 14155776 | tf_op jit(solution)/shard_map/reshape | solution.py:76
  99.1 8.4 %copy.49 = bf16[288,16,768]{2,0,1:T(8,128)(2,1)} copy(bf16[288,16,768]{2,1,0:T(8,128)(2,1)} %reshape.91) | data formatting | bytes 14155776 | tf_op jit(solution)/shard_map/reshape | solution.py:76
  107.4 3.7 gather_fusion.5
  111.1 3.7 gather_fusion.4
  114.8 5.2 fusion.6
  129.8 324.3 %all-gather.9.cloned.1.call-done = f32[32,768,768]{2,1,0:T(8,128)} async-done(((f32[4,768,768]{2,1,0:T(8,128)}), f32[32,768,768]{2,1,0:T(8,128)}) %all-gather.9.cloned.1.call-update) | async-done | bytes 75497488 | tf_op jit(solution)/shard_map/all_gather | solution.py:10
  454.1 28.2 %reduce_sum.9 = f32[4,768,768]{2,1,0:T(8,128)} reduce(f32[8,4,768,768]{3,2,1,0:T(8,128)} %bitcast.5, f32[]{:T(128)} %constant.16.clone.1), dimensions={0}, to_apply=%region_0.0 | reduce | flops 16515072 | bytes 84934656 | tf_op jit(solution)/shard_map/reduce_sum | solution.py:10
  482.3 12.5 %reshape.92 = f32[4,2,384,2,384]{4,3,2,1,0:T(2,128)} reshape(f32[4,768,768]{2,1,0:T(8,128)} %reduce_sum.9) | data formatting | bytes 18874368 | tf_op jit(solution)/shard_map/reshape | solution.py:52
  494.8 14.7 %copy.52 = f32[4,2,384,2,384]{2,4,3,1,0:T(8,128)} copy(f32[4,2,384,2,384]{4,3,2,1,0:T(2,128)} %reshape.92) | data formatting | bytes 18874368 | tf_op jit(solution)/shard_map/reshape | solution.py:52
  509.5 9.9 %fusion.1 = bf16[4,2,384,2,384]{4,2,3,1,0:T(8,128)(2,1)} fusion(f32[4,2,384,2,384]{2,4,3,1,0:T(8,128)} %copy.52, f32[4,2,384,2,384]{4,3,2,1,0:T(2,128)} %reshape.92, f32[384]{0:T(512)S(1)} %copy-done.2, f32[4,2,384,2]{2,3,1,0:T(2,128)} %broadcast_subtract_fusion), kind=kLoop, calls=%fused_computation.9 | loop fusion | flops 11796480 | bytes 23619072 | tf_op jit(solution)/shard_map/convert_element_type | solution.py:61
  519.5 9.4 %copy.53 = bf16[4,2,384,2,384]{4,3,2,1,0:T(2,128)(2,1)} copy(bf16[4,2,384,2,384]{4,2,3,1,0:T(8,128)(2,1)} %fusion.1) | data formatting | bytes 9437184 | tf_op jit(solution)/shard_map/convert_element_type | solution.py:61
  528.9 6.7 copy.64
  535.6 11.4 %reshape.94 = bf16[4,768,768]{2,1,0:T(8,128)(2,1)} reshape(bf16[4,2,384,2,384]{4,3,2,1,0:T(2,128)(2,1)} %copy.53) | data formatting | bytes 9437184 | tf_op jit(solution)/shard_map/reshape | solution.py:61
  547.0 5.7 convolution_bitcast_fusion.1
  552.7 1.7 convolution_bitcast_fusion.2
  555.7 13.1 %fusion.3 = f32[288,768,16]{1,2,0:T(8,128)} fusion(f32[288,4,768]{2,0,1:T(8,128)} %convolution_bitcast_fusion.1, s32[4]{0:T(128)S(1)} %copy-done.4), kind=kOutput, calls=%fused_computation.12 | convolution fusion | flops 169869376 | bytes 17694736 | tf_op jit(solution)/shard_map/sk,psx->pkx/dot_general | solution.py:104
  568.8 5.8 convolution_bitcast_fusion
  574.6 22.6 %all-reduce.8.cloned.1.call-done = f32[128,3,384]{2,1,0:T(4,128)} async-done(((f32[128,3,384]{2,1,0:T(4,128)}), f32[128,3,384]{2,1,0:T(4,128)}) %all-reduce.8.cloned.1.call-update) | async-done | bytes 589840
  598.9 15.4 %add_bitcast_fusion = f32[288,16,768]{2,1,0:T(8,128)} fusion(f32[288,768,16]{1,2,0:T(8,128)} %fusion.3, f32[288,4,768]{2,0,1:T(8,128)} %convolution_bitcast_fusion, s32[4]{0:T(128)S(1)} %copy-done.6), kind=kOutput, calls=%fused_computation.6 | convolution fusion | flops 173408320 | bytes 31850512 | tf_op jit(solution)/shard_map/sk,psx->pkx/dot_general | solution.py:106
  614.3 18.3 %copy.56 = f32[288,16,768]{2,0,1:T(8,128)} copy(f32[288,16,768]{2,1,0:T(8,128)} %add_bitcast_fusion) | data formatting | bytes 28311552 | tf_op jit(solution)/shard_map/add | solution.py:104
  636.4 5.6 all-reduce.10.cloned.1.call-done
  642.8 14.0 %all-reduce.3 = f32[8,3,384]{2,1,0:T(4,128)S(1)} all-reduce(f32[8,3,384]{2,1,0:T(4,128)S(1)} %constant_dynamic-slice_fusion.1), channel_id=9, replica_groups=mesh['orow_0'=4,'orow_1'=4,'ocol_0'=4,'ocol_1'=2] {'ocol_0'}, use_global_device_ids=true, to_apply=%region_4.6.clone | all-reduce | flops 9216 | bytes 73728
  656.8 9.2 %all-reduce.4 = f32[2,3,384]{2,1,0:T(4,128)S(1)} all-reduce(f32[2,3,384]{2,1,0:T(4,128)S(1)} %constant_dynamic-slice_fusion), channel_id=10, replica_groups=mesh['orow_0'=4,'orow_1'=4,'ocol_0'=4,'ocol_1'=2] {'ocol_1'}, use_global_device_ids=true, to_apply=%region_5.7.clone | all-reduce | flops 2304 | bytes 18432
  666.7 1.8 all_gather.33
  668.5 10.1 %all-gather.1 = f32[8,3,384]{2,1,0:T(4,128)S(1)} all-gather(f32[2,3,384]{2,1,0:T(4,128)S(1)} %all_gather.33), channel_id=3, replica_groups=mesh['orow_0'=4,'orow_1'=4,'ocol_0'=4,'ocol_1'=2] {'ocol_0'}, dimensions={0}, use_global_device_ids=true | all-gather | bytes 46080 | tf_op jit(solution)/shard_map/all_gather | solution.py:33
  678.7 11.2 %all-gather.2 = f32[16,2,3,384]{3,1,2,0:T(2,128)S(1)} all-gather(f32[4,2,3,384]{3,1,2,0:T(2,128)S(1)} %copy.59), channel_id=4, replica_groups=mesh['orow_0'=4,'orow_1'=4,'ocol_0'=4,'ocol_1'=2] {'orow_1'}, dimensions={0}, use_global_device_ids=true | all-gather | bytes 184320 | tf_op jit(solution)/shard_map/all_gather | solution.py:33
  689.9 15.1 %all-gather.3 = f32[16,4,2,3,384]{4,1,3,2,0:T(4,128)S(1)} all-gather(f32[4,4,2,3,384]{4,1,3,2,0:T(4,128)S(1)} %copy.60), channel_id=5, replica_groups=mesh['orow_0'=4,'orow_1'=4,'ocol_0'=4,'ocol_1'=2] {'orow_0'}, dimensions={0}, use_global_device_ids=true | all-gather | bytes 737280 | tf_op jit(solution)/shard_map/all_gather | solution.py:33
  706.5 45.8 %reduce-scatter.4.cloned.1.call-done = f32[288,1,768]{2,0,1:T(8,128)} async-done(((f32[288,16,768]{2,0,1:T(8,128)}), f32[288,1,768]{2,0,1:T(8,128)}) %reduce-scatter.4.cloned.1.call-update) | async-done | bytes 884752
  752.3 2.6 reshape.95
  (64 shorter events, 21.6 us)
Async XLA Ops:
  7.2 4.0 copy-start
  7.2 72.1 %all-gather.7.cloned.1.call-start = ((), (), s32[]{:S(2)}) async-start(), calls=%async_computation.1 | async-start | bytes 7520256 | tf_op jit(solution)/shard_map/all_gather | solution.py:75
  11.0 443.0 %all-gather.9.cloned.1.call-start = ((), (), s32[]{:S(2)}) async-start(), calls=%async_computation.2 | async-start | bytes 84934656 | tf_op jit(solution)/shard_map/all_gather | solution.py:10
  11.8 76.0 %copy-start.3 = (s32[4]{0:T(128)}, s32[4]{0:T(128)S(1)}, u32[]{:S(2)}) copy-start(s32[4]{0:T(128)S(1)} %gather_fusion.1) | copy-start | bytes 52
  13.1 74.7 %copy-start.5 = (s32[4]{0:T(128)}, s32[4]{0:T(128)S(1)}, u32[]{:S(2)}) copy-start(s32[4]{0:T(128)S(1)} %gather_fusion) | copy-start | bytes 52
  120.0 477.2 %all-reduce.8.cloned.1.call-start = ((), (), s32[]{:S(2)}) async-start(), calls=%async_computation.3 | async-start | bytes 1572864
  494.8 14.7 %copy-start.2 = (f32[384]{0:T(512)S(1)}, f32[384]{0:T(512)}, u32[]{:S(2)}) copy-start(f32[384]{0:T(512)} %param.11) | copy-start | bytes 4612
  547.0 8.7 %copy-start.4 = (s32[4]{0:T(128)S(1)}, s32[4]{0:T(128)}, u32[]{:S(2)}) copy-start(s32[4]{0:T(128)} %copy-done.3) | copy-start | bytes 52
  555.6 86.4 %all-reduce.10.cloned.1.call-start = ((), (), s32[]{:S(2)}) async-start(), calls=%async_computation.4 | async-start | bytes 393216
  568.8 30.1 %copy-start.6 = (s32[4]{0:T(128)S(1)}, s32[4]{0:T(128)}, u32[]{:S(2)}) copy-start(s32[4]{0:T(128)} %copy-done.5) | copy-start | bytes 52
  598.8 153.5 %reduce-scatter.4.cloned.1.call-start = ((), (), s32[]{:S(2)}) async-start(), calls=%async_computation.5 | async-start | bytes 15040512
  632.6 0.7 copy-start.9
  632.6 1.2 copy-start.8
  632.6 1.9 copy-start.7
  633.3 121.6 %copy-start.1 = (s32[64,1]{0,1:T(1,128)S(1)}, s32[64,1]{0,1:T(1,128)}, u32[]{:S(2)}) copy-start(s32[64,1]{0,1:T(1,128)} %param.12) | copy-start | bytes 772
Sparse Core Ops, SparseCore 0:
  11.2 68.0 all-gather.6
  120.1 333.9 all-gather.8
  555.7 41.3 all-reduce.7
  599.9 42.0 all-reduce.9
  645.3 106.9 reduce-scatter.3
